TPU v7x, 32 devices: a whole 2x2x4 slice. The times are simulated.
32 devices in a mesh: blk: 8 (over z, core), tenant: 4 (over y, x).
Axes of the slice: x: 2, y: 2, z: 4, core: 2. Of those that a mesh axis runs over, the one named last changes fastest.
Arguments:
- history_u: bfloat16 [4, 1024, 4096], P('tenant', 'blk'), may hold values from -6 to 6
- span_gate: bfloat16 [4, 64, 4096], P('tenant', 'blk'), may hold values from -6 to 6
- span_key: bfloat16 [4, 64, 4096], P('tenant', 'blk'), may hold values from -6 to 6
- span_value: bfloat16 [4, 64, 4096], P('tenant', 'blk'), may hold values from -6 to 6
- filter_taps: bfloat16 [1088, 256], P(('blk', 'tenant'))
- skip_bias: bfloat16 [4096], P(('blk', 'tenant')), may hold values from -6 to 6
- lengths: int32 [4], P('tenant'), may hold values from 1 to 1024, as said below
- page_owner: int32 [4, 8, 1], P('tenant'), may hold values from 0 to 7; in each aligned block of 8 rows (0 to 7, 8 to 15, ..., all dimensions but the last counted through in order) at most 2 rows name the same one
Outputs:
- mixed: bfloat16 [4, 64, 4096], P('tenant', 'blk')
- new_pool: bfloat16 [4, 128, 4096], P('tenant', 'blk')
Inputs may be any that keep to these rules, and one draw needn't show every extreme that they name: `lengths`: lengths are at least 1, and some tenant uses all 1024 cached positions in every draw. `page_owner`: among the 8 pages of one tenant no device is named more than 2 times, and some device is named exactly 2 times.
All inputs are finite; a program needn't handle non-finite values.
Results may differ from a plain program's by a relative error of at most 0.0044.
Values may be sent and summed in bfloat16 or wider, within the bound.
No kernel may reach another device: no remote copies, remote signals or barrier semaphores. Data moves between devices by JAX's collectives and lax.ppermute only.
A program may use at most 128 MiB of HBM per device.

v0:
```python
import jax
import jax.numpy as jnp
from jax import lax
from jax.sharding import PartitionSpec as P

PAGE = 8
PAGES_DEV = 1
MOST = 2


def toeplitz(window, tile_rows, groups):
    reversed_taps = jnp.transpose(window[::-1])
    repeated = jnp.tile(reversed_taps, (1, tile_rows))
    trimmed = repeated[:, tile_rows - 1 : tile_rows - 1 + tile_rows * (2 * tile_rows - 2)]
    return trimmed.reshape(groups, tile_rows, 2 * tile_rows - 2)[:, :, :tile_rows]


def tile_table(padded_filter, starts, tile_rows, groups):

    def one_window(start):
        window = lax.dynamic_slice_in_dim(padded_filter, start, 2 * tile_rows - 1, 0)
        return toeplitz(window, tile_rows, groups)

    return jax.vmap(one_window)(starts)


def blocked_convolution(table, sources_reversed, target_blocks, source_blocks):

    def per_target(target_index):
        tiles = lax.dynamic_slice_in_dim(table, target_index, source_blocks, 0)
        return jnp.einsum(
            "mgab,mbgc->agc", tiles, sources_reversed, preferred_element_type=jnp.float32
        )

    return lax.map(per_target, jnp.arange(target_blocks, dtype=jnp.int32))


def per_device(
    history_u, span_gate, span_key, span_value, filter_taps, skip_bias, lengths, page_owner
):
    cycle_size = lax.axis_size("blk")
    own_index = lax.axis_index("blk")
    history = history_u[0]
    gate_rows = span_gate[0]
    history_rows, width = history.shape
    span_rows = gate_rows.shape[0]
    span_total = span_rows * cycle_size
    groups = filter_taps.shape[1]
    group_size = width // groups
    taps_all, bias_all = (
        lax.all_gather(filter_taps, ("blk", "tenant"), axis=0, tiled=True),
        lax.all_gather(skip_bias, ("blk", "tenant"), axis=0, tiled=True),
    )
    length = lengths[0]
    own_rows = (span_key[0].astype(jnp.float32) * span_value[0].astype(jnp.float32)).astype(
        jnp.bfloat16
    )
    tile_rows = min(32, history_rows, span_total)
    target_blocks = span_total // tile_rows
    column_history, column_span = (
        lax.all_to_all(history, "blk", split_axis=1, concat_axis=0, tiled=True),
        lax.all_to_all(own_rows, "blk", split_axis=1, concat_axis=0, tiled=True),
    )
    column_width = width // cycle_size
    local_groups = column_width // group_size
    full_rows = column_history.shape[0]
    filter_rows_all = full_rows + span_total
    taps_local = lax.dynamic_slice_in_dim(taps_all, own_index * local_groups, local_groups, 1)
    masked_columns = jnp.where(
        jnp.arange(full_rows, dtype=jnp.int32)[:, None] < length,
        column_history,
        jnp.zeros_like(column_history),
    )
    sequence = jnp.concatenate(
        [masked_columns, jnp.zeros((span_total, column_width), jnp.bfloat16)], axis=0
    )
    sequence = lax.dynamic_update_slice(sequence, column_span, (length, jnp.int32(0)))
    source_blocks = filter_rows_all // tile_rows
    padded_filter = jnp.concatenate(
        [jnp.zeros((filter_rows_all, local_groups), jnp.bfloat16), taps_local], axis=0
    )
    offsets = jnp.arange(target_blocks + source_blocks - 1, dtype=jnp.int32) - (source_blocks - 1)
    starts = length + offsets * tile_rows - (tile_rows - 1) + filter_rows_all
    table = tile_table(padded_filter, starts, tile_rows, local_groups)
    sources_reversed = sequence.reshape(source_blocks, tile_rows, local_groups, group_size)[::-1]
    column_out = blocked_convolution(table, sources_reversed, target_blocks, source_blocks).reshape(
        span_total, column_width
    )
    convolved = lax.all_to_all(column_out, "blk", split_axis=0, concat_axis=1, tiled=True)
    mixed = (
        gate_rows.astype(jnp.float32)
        * (convolved + bias_all.astype(jnp.float32)[None, :] * own_rows.astype(jnp.float32))
    ).astype(jnp.bfloat16)
    owners = page_owner[0, :, 0]
    page_count = owners.shape[0]
    onehot = (owners[:, None] == jnp.arange(cycle_size, dtype=jnp.int32)[None, :]).astype(jnp.int32)
    before = jnp.cumsum(onehot, axis=0) - onehot
    slot_rank = jnp.sum(before * onehot, axis=1)
    selector = (
        (owners[None, :] == own_index)
        & (slot_rank[None, :] == jnp.arange(MOST, dtype=jnp.int32)[:, None])
    ).astype(jnp.bfloat16)
    local_pages = own_rows.reshape(PAGES_DEV, PAGE * width)
    targets_of = lax.dynamic_slice_in_dim(owners, own_index * PAGES_DEV, PAGES_DEV, 0)
    send_mask = targets_of[None, :] == jnp.arange(cycle_size, dtype=jnp.int32)[:, None]
    outgoing = jnp.where(
        send_mask[:, :, None], local_pages[None, :, :], jnp.zeros((), jnp.bfloat16)
    )
    incoming = lax.all_to_all(outgoing, "blk", split_axis=0, concat_axis=0, tiled=True)
    arrived = incoming.reshape(page_count, PAGE * width)
    new_pool = jnp.dot(selector, arrived, preferred_element_type=jnp.float32).astype(jnp.bfloat16)
    return (mixed[None], new_pool.reshape(MOST * PAGE, width)[None])


def solution(mesh):
    return jax.shard_map(
        per_device,
        mesh=mesh,
        in_specs=(
            P("tenant", "blk", None),
            P("tenant", "blk", None),
            P("tenant", "blk", None),
            P("tenant", "blk", None),
            P(("blk", "tenant"), None),
            P(("blk", "tenant")),
            P("tenant"),
            P("tenant", None, None),
        ),
        out_specs=(P("tenant", "blk", None), P("tenant", "blk", None)),
        check_vma=False,
    )
```

profile of v0, /device:TPU:0, one launch (start us, length us, event | category | flops | bytes accessed | tf_op | source)
XLA Modules:
  0.0 384.5 jit_solution(1890351494734139457)
XLA Ops:
  0.6 1.3 constant_dynamic-slice_fusion.1
  2.6 1.5 multiply_convert_fusion.1
  5.0 0.9 broadcast_select_fusion
  6.5 3.8 reduce
  10.3 1.2 reshape.183
  11.4 6.3 %all-to-all-start.3 = ((bf16[8,2,16384]{2,1,0:T(2,128)(2,1)}), bf16[8,2,16384]{2,1,0:T(2,128)(2,1)S(1)}, u32[]{:S(2)}, u32[]{:S(2)}) async-start(bf16[8,2,16384]{2,1,0:T(2,128)(2,1)} %reshape.183), calls=%async_computation.3 | async-start | bytes 1048576 | tf_op jit(solution)/shard_map/all_to_all | solution.py:109
  17.8 74.8 %all-gather = bf16[32,34,256]{2,1,0:T(8,128)(2,1)S(1)} all-gather(bf16[1,34,256]{2,1,0:T(8,128)(2,1)} %bitcast.67), channel_id=1, replica_groups=mesh['blk'=8,'tenant'=4] {'blk','tenant'}, dimensions={0}, use_global_device_ids=true | all-gather | bytes 574464 | tf_op jit(solution)/shard_map/all_gather | solution.py:51
  93.4 1.3 copy.31
  95.0 3.7 all-to-all-start
  98.8 65.2 %while.12 = (s32[]{:T(128)}, bf16[2176,32]{1,0:T(8,128)(2,1)S(1)}, s32[35,2]{0,1:T(2,128)S(1)}, bf16[35,63,32]{2,1,0:T(8,128)(2,1)}, s32[]{:T(128)}) while((s32[]{:T(128)}, bf16[2176,32]{1,0:T(8,128)(2,1)S(1)}, s32[35,2]{0,1:T(2,128)S(1)}, bf16[35,63,32]{2,1,0:T(8,128)(2,1)}, s32[]{:T(128)}) %tuple.37), condition=%wide.while_cond, body=%wide.while_body.sunk | while | flops 2 | bytes 21529 | solution.py:21
  99.4 1.3 bitcast_dynamic-update-slice_fusion.2
  101.3 1.2 bitcast_dynamic-update-slice_fusion.2
  103.1 1.2 bitcast_dynamic-update-slice_fusion.2
  105.0 1.2 bitcast_dynamic-update-slice_fusion.2
  106.8 1.3 bitcast_dynamic-update-slice_fusion.2
  108.7 1.2 bitcast_dynamic-update-slice_fusion.2
  110.6 1.2 bitcast_dynamic-update-slice_fusion.2
  112.4 1.3 bitcast_dynamic-update-slice_fusion.2
  114.3 1.2 bitcast_dynamic-update-slice_fusion.2
  116.2 1.2 bitcast_dynamic-update-slice_fusion.2
  118.0 1.2 bitcast_dynamic-update-slice_fusion.2
  119.9 1.3 bitcast_dynamic-update-slice_fusion.2
  121.8 1.2 bitcast_dynamic-update-slice_fusion.2
  123.6 1.2 bitcast_dynamic-update-slice_fusion.2
  125.5 1.2 bitcast_dynamic-update-slice_fusion.2
  127.3 1.3 bitcast_dynamic-update-slice_fusion.2
  129.2 1.2 bitcast_dynamic-update-slice_fusion.2
  131.1 1.2 bitcast_dynamic-update-slice_fusion.2
  132.9 1.2 bitcast_dynamic-update-slice_fusion.2
  134.8 1.3 bitcast_dynamic-update-slice_fusion.2
  136.7 1.2 bitcast_dynamic-update-slice_fusion.2
  138.5 1.3 bitcast_dynamic-update-slice_fusion.2
  140.4 1.2 bitcast_dynamic-update-slice_fusion.2
  142.2 1.2 bitcast_dynamic-update-slice_fusion.2
  144.1 1.2 bitcast_dynamic-update-slice_fusion.2
  146.0 1.2 bitcast_dynamic-update-slice_fusion.2
  147.8 1.3 bitcast_dynamic-update-slice_fusion.2
  149.7 1.3 bitcast_dynamic-update-slice_fusion.2
  151.6 1.2 bitcast_dynamic-update-slice_fusion.2
  153.4 1.2 bitcast_dynamic-update-slice_fusion.2
  155.3 1.2 bitcast_dynamic-update-slice_fusion.2
  157.1 1.2 bitcast_dynamic-update-slice_fusion.2
  159.0 1.2 bitcast_dynamic-update-slice_fusion.2
  160.9 1.2 bitcast_dynamic-update-slice_fusion.2
  162.7 1.2 bitcast_dynamic-update-slice_fusion.2
  164.0 2.3 rev.6
  166.6 4.7 %tile.4 = bf16[35,32,32,63]{3,2,1,0:T(8,128)(2,1)} broadcast(bf16[35,32,63]{2,1,0:T(8,128)(2,1)S(1)} %copy.30), dimensions={0,1,3} | broadcast | bytes 4656960 | tf_op jit(solution)/shard_map/vmap()/tile | solution.py:13
  171.3 16.1 %tile.10 = bf16[35,32,2016]{2,1,0:T(8,128)(2,1)} reshape(bf16[35,32,32,63]{3,2,1,0:T(8,128)(2,1)} %tile.4) | data formatting | bytes 9031680 | tf_op jit(solution)/shard_map/vmap()/tile | solution.py:13
  187.4 6.9 %slice.19 = bf16[35,32,1984]{2,1,0:T(8,128)(2,1)} slice(bf16[35,32,2016]{2,1,0:T(8,128)(2,1)} %tile.10), slice={[0:35], [0:32], [31:2015]} | slice | bytes 8888320 | tf_op jit(solution)/shard_map/vmap()/slice | solution.py:14
  194.4 31.4 %reshape.155 = bf16[35,32,32,62]{3,2,1,0:T(8,128)(2,1)} reshape(bf16[35,32,1984]{2,1,0:T(8,128)(2,1)} %slice.19) | data formatting | bytes 8888320 | tf_op jit(solution)/shard_map/vmap()/reshape | solution.py:15
  225.8 14.3 %copy.34 = bf16[35,32,32,32]{0,2,3,1:T(8,128)(2,1)} copy(bf16[35,32,32,32]{3,2,1,0:T(8,128)(2,1)} %bitcast.60) | data formatting | bytes 4587520 | tf_op jit(solution)/shard_map/while | solution.py:35
  240.1 66.1 %all-gather.1 = bf16[32,1,128]{2,1,0:T(2,128)(2,1)S(1)} all-gather(bf16[1,1,128]{2,1,0:T(2,128)(2,1)S(1)} %bitcast.70), channel_id=1, replica_groups=mesh['blk'=8,'tenant'=4] {'blk','tenant'}, dimensions={0}, use_global_device_ids=true | all-gather | bytes 8448 | tf_op jit(solution)/shard_map/all_gather | solution.py:52
  307.1 3.6 all-to-all-start.1
  311.5 4.8 %all-to-all-done.1 = bf16[8,8,512]{2,0,1:T(8,128)(2,1)S(1)} async-done(((bf16[8,8,512]{2,0,1:T(8,128)(2,1)}), bf16[8,8,512]{2,0,1:T(8,128)(2,1)S(1)}, u32[]{:S(2)}, u32[]{:S(2)}) %all-to-all-start.1) | async-done | bytes 65568 | tf_op jit(solution)/shard_map/all_to_all | solution.py:62
  317.4 4.8 %reshape.156 = bf16[34,32,32,16]{1,0,3,2:T(8,128)(2,1)} reshape(bf16[1088,512]{0,1:T(8,128)(2,1)S(1)} %copy.33) | data formatting | bytes 2228224 | tf_op jit(solution)/shard_map/reshape | solution.py:85
  322.2 20.3 %rev.7 = bf16[34,32,32,16]{1,0,3,2:T(8,128)(2,1)} reverse(bf16[34,32,32,16]{1,0,3,2:T(8,128)(2,1)} %reshape.156), dimensions={0} | reverse | bytes 2228224 | tf_op jit(solution)/shard_map/rev | solution.py:85
  342.5 8.7 %copy.35 = bf16[34,32,32,16]{0,3,1,2:T(8,128)(2,1)} copy(bf16[34,32,32,16]{1,0,3,2:T(8,128)(2,1)} %rev.7) | data formatting | bytes 2228224 | tf_op jit(solution)/shard_map/while | solution.py:35
  351.2 19.5 %while.11 = (s32[]{:T(128)}, f32[2,32,32,16]{1,3,2,0:T(8,128)S(1)}, s32[2]{0:T(128)S(1)}, bf16[35,32,32,32]{0,2,3,1:T(8,128)(2,1)}, bf16[34,32,32,16]{0,3,1,2:T(8,128)(2,1)}, /*index=5*/s32[]{:T(128)}, s32[]{:T(128)}, s32[]{:T(128)}) while((s32[]{:T(128)}, f32[2,32,32,16]{1,3,2,0:T(8,128)S(1)}, s32[2]{0:T(128)S(1)}, ...), condition=%wide.region_1.2_spmd, body=%wide.region_0.1_spmd.sunk | while | flops 35651588 | bytes 3670155 | solution.py:35
  354.0 7.0 %fusion.23 = f32[2,32,32,16]{1,3,2,0:T(8,128)S(1)} fusion(f32[2,32,32,16]{1,3,2,0:T(8,128)S(1)} %get-tuple-element.156, s32[]{:T(128)} %get-tuple-element.155, bf16[34,32,32,16]{0,3,1,2:T(8,128)(2,1)} %get-tuple-element.167, bf16[35,32,32,32]{0,2,3,1:T(8,128)(2,1)} %get-tuple-element.166, s32[]{:T(128)S(6)} %select_n.48), kind=kOutput, calls=%fused_computation.3.clone.1 | convolution fusion | flops 35651584 | bytes 3670024 | tf_op jit(solution)/shard_map/while/body/eval_jaxpr/mgab,mbgc->agc/dot_general | solution.py:31
  363.7 7.0 %fusion.23 = f32[2,32,32,16]{1,3,2,0:T(8,128)S(1)} fusion(f32[2,32,32,16]{1,3,2,0:T(8,128)S(1)} %get-tuple-element.156, s32[]{:T(128)} %get-tuple-element.155, bf16[34,32,32,16]{0,3,1,2:T(8,128)(2,1)} %get-tuple-element.167, bf16[35,32,32,32]{0,2,3,1:T(8,128)(2,1)} %get-tuple-element.166, s32[]{:T(128)S(6)} %select_n.48), kind=kOutput, calls=%fused_computation.3.clone.1 | convolution fusion | flops 35651584 | bytes 3670024 | tf_op jit(solution)/shard_map/while/body/eval_jaxpr/mgab,mbgc->agc/dot_general | solution.py:31
  371.6 1.3 all_to_all.50
  372.9 3.4 all-to-all-start.2
  377.7 5.3 %all-to-all-done.2 = f32[8,8,512]{2,1,0:T(8,128)S(1)} async-done(((f32[8,8,512]{2,1,0:T(8,128)}), f32[8,8,512]{2,1,0:T(8,128)S(1)}, u32[]{:S(2)}, u32[]{:S(2)}) %all-to-all-start.2) | async-done | bytes 131104 | tf_op jit(solution)/shard_map/all_to_all | solution.py:89
  383.0 1.5 multiply_convert_fusion
  (111 shorter events, 30.6 us)
Async XLA Ops:
  0.6 92.8 %copy-start = (bf16[1,128,4096]{2,1,0:T(8,128)(2,1)S(1)}, bf16[1,128,4096]{2,1,0:T(8,128)(2,1)}, u32[]{:S(2)}) copy-start(bf16[1,128,4096]{2,1,0:T(8,128)(2,1)} %param.10) | copy-start | bytes 3145732
  11.4 83.6 %all-to-all-start.3 = ((bf16[8,2,16384]{2,1,0:T(2,128)(2,1)}), bf16[8,2,16384]{2,1,0:T(2,128)(2,1)S(1)}, u32[]{:S(2)}, u32[]{:S(2)}) async-start(bf16[8,2,16384]{2,1,0:T(2,128)(2,1)} %reshape.183), calls=%async_computation.3 | async-start | bytes 1048576 | tf_op jit(solution)/shard_map/all_to_all | solution.py:109
  95.0 212.0 %all-to-all-start = ((bf16[128,8,512]{0,2,1:T(8,128)(2,1)}), bf16[128,8,512]{0,2,1:T(8,128)(2,1)S(1)}, u32[]{:S(2)}, u32[]{:S(2)}) async-start(bf16[128,8,512]{0,2,1:T(8,128)(2,1)} %bitcast.8), calls=%async_computation | async-start | bytes 2097152 | tf_op jit(solution)/shard_map/all_to_all | solution.py:61
  225.8 14.3 %copy-start.4 = (bf16[128]{0:T(256)(128)(2,1)S(1)}, bf16[128]{0:T(256)(128)(2,1)}, u32[]{:S(2)}) copy-start(bf16[128]{0:T(256)(128)(2,1)} %param.15) | copy-start | bytes 772
  225.8 80.4 %copy-start.3 = (s32[1,8,1]{1,2,0:T(1,128)S(1)}, s32[1,8,1]{1,2,0:T(1,128)}, u32[]{:S(2)}) copy-start(s32[1,8,1]{1,2,0:T(1,128)} %param.17) | copy-start | bytes 100
  307.1 9.2 %all-to-all-start.1 = ((bf16[8,8,512]{2,0,1:T(8,128)(2,1)}), bf16[8,8,512]{2,0,1:T(8,128)(2,1)S(1)}, u32[]{:S(2)}, u32[]{:S(2)}) async-start(bf16[8,8,512]{2,0,1:T(8,128)(2,1)} %bitcast.11), calls=%async_computation.1 | async-start | bytes 131072 | tf_op jit(solution)/shard_map/all_to_all | solution.py:62
  342.5 8.7 %copy-start.1 = (f32[2,32,32,16]{1,3,2,0:T(8,128)S(1)}, f32[2,32,32,16]{1,3,2,0:T(8,128)}, u32[]{:S(2)}) copy-start(f32[2,32,32,16]{1,3,2,0:T(8,128)} %custom-call) | copy-start | bytes 393220
  351.2 31.8 %copy-start.2 = (bf16[1,8,4096]{2,1,0:T(8,128)(2,1)S(1)}, bf16[1,8,4096]{2,1,0:T(8,128)(2,1)}, u32[]{:S(2)}) copy-start(bf16[1,8,4096]{2,1,0:T(8,128)(2,1)} %param.11) | copy-start | bytes 196612
  372.9 10.1 %all-to-all-start.2 = ((f32[8,8,512]{2,1,0:T(8,128)}), f32[8,8,512]{2,1,0:T(8,128)S(1)}, u32[]{:S(2)}, u32[]{:S(2)}) async-start(f32[8,8,512]{2,1,0:T(8,128)} %all_to_all.50), calls=%async_computation.2 | async-start | bytes 262144 | tf_op jit(solution)/shard_map/all_to_all | solution.py:89
where the time goes:
time: 387 us; the launch traced here: 385 us
  local copies, waits for them, and re-layouts  187 us (48%)
  blocking collectives  141 us (36%)
  starting transfers between devices  17 us (4%)
  matrix products  14.7 us (4%)
  waiting for transfers between devices  10.1 us (3%)
  other arithmetic  8.95 us (2%)
  loops' own time  4.23 us (1%)
    all_gather x1, blocking collectives, per_device(): lax.all_gather(filter_taps, ('blk', 'tenant'), axis=0, tiled=True)  74.8 us
    all_gather x1, blocking collectives, per_device(): lax.all_gather(skip_bias, ('blk', 'tenant'), axis=0, tiled=True)  66.1 us
    gather x105, local copies, waits for them, and re-layouts  65.1 us
    reshape x1, local copies, waits for them, and re-layouts, toeplitz(): trimmed.reshape(groups, tile_rows, 2 * tile_rows - 2)[:, :, :tile_rows]  31.4 us
    while x3, local copies, waits for them, and re-layouts, blocked_convolution(): return lax.map(per_target, jnp.arange(target_blocks, dtype=jnp.int32))  23.9 us
    another operation x2, local copies, waits for them, and re-layouts, toeplitz(): repeated = jnp.tile(reversed_taps, (1, tile_rows))  20.8 us
    rev x1, local copies, waits for them, and re-layouts, per_device(): sequence.reshape(source_blocks, tile_rows, local_groups, group_size)[::-1]  20.3 us
    dot_general x2, matrix products, per_target(): jnp.einsum('mgab,mbgc->agc', tiles, sources_reversed, preferred_element_t...  14 us
  transfers between devices with their start and end apart: 4, of which 2 were waited for; matrix products, arithmetic and copies ran while one was open for 38% of the time, Pallas kernels for 0%

commit v1 on v0

--- a/solution.py
+++ b/solution.py
@@ -86,7 +86,10 @@
     column_out = blocked_convolution(table, sources_reversed, target_blocks, source_blocks).reshape(
         span_total, column_width
     )
-    convolved = lax.all_to_all(column_out, "blk", split_axis=0, concat_axis=1, tiled=True)
+    convolved = jnp.concatenate(
+        lax.all_to_all(jnp.stack(jnp.split(column_out, lax.axis_size("blk"), axis=0)), "blk", 0, 0),
+        axis=1,
+    )
     mixed = (
         gate_rows.astype(jnp.float32)
         * (convolved + bias_all.astype(jnp.float32)[None, :] * own_rows.astype(jnp.float32))

time: 387 us -> 400 us (1.034)
  local copies, waits for them, and re-layouts: 187 us -> 201 us
    dynamic_update_slice x0 -> x2, local copies, waits for them, and re-layouts: none -> 11 us  [blocked_convolution(): return lax.map(per_target, jnp.arange(target_blocks, dtype=jnp.int32))]
    unnamed x15 -> x22, local copies, waits for them, and re-layouts: 4.04 us -> 8.28 us
    while x3 -> x2, local copies, waits for them, and re-layouts: 23.9 us -> 23 us  [blocked_convolution(): return lax.map(per_target, jnp.arange(target_blocks, dtype=jnp.int32))]
  transfers between devices with their start and end apart: 4 -> 4, of which waited for: 2 -> 2; matrix products, arithmetic and copies ran while one was open for 38% -> 36% of each run, Pallas kernels for 0% -> 0%
where the time goes in v1:
time: 400 us; the launch traced here: 398 us
  local copies, waits for them, and re-layouts  201 us (50%)
  blocking collectives  141 us (35%)
  starting transfers between devices  17 us (4%)
  matrix products  14.7 us (4%)
  waiting for transfers between devices  10.1 us (3%)
  other arithmetic  8.95 us (2%)
    all_gather x1, blocking collectives, per_device(): lax.all_gather(filter_taps, ('blk', 'tenant'), axis=0, tiled=True)  74.8 us
    all_gather x1, blocking collectives, per_device(): lax.all_gather(skip_bias, ('blk', 'tenant'), axis=0, tiled=True)  66.1 us
    gather x105, local copies, waits for them, and re-layouts  62.4 us
    reshape x1, local copies, waits for them, and re-layouts, toeplitz(): trimmed.reshape(groups, tile_rows, 2 * tile_rows - 2)[:, :, :tile_rows]  31.4 us
    while x2, local copies, waits for them, and re-layouts, blocked_convolution(): return lax.map(per_target, jnp.arange(target_blocks, dtype=jnp.int32))  23 us
    another operation x2, local copies, waits for them, and re-layouts, toeplitz(): repeated = jnp.tile(reversed_taps, (1, tile_rows))  20.9 us
    rev x1, local copies, waits for them, and re-layouts, per_device(): sequence.reshape(source_blocks, tile_rows, local_groups, group_size)[::-1]  20.3 us
    dot_general x2, matrix products, per_target(): jnp.einsum('mgab,mbgc->agc', tiles, sources_reversed, preferred_element_t...  14 us
  transfers between devices with their start and end apart: 4, of which 2 were waited for; matrix products, arithmetic and copies ran while one was open for 36% of the time, Pallas kernels for 0%

profile of v1, /device:TPU:0, one launch (start us, length us, event | category | flops | bytes accessed | tf_op | source)
XLA Modules:
  0.0 397.7 jit_solution(7861492185933958684)
XLA Ops:
  0.6 1.3 constant_dynamic-slice_fusion.1
  2.6 1.5 multiply_convert_fusion.1
  6.5 3.8 reduce
  11.4 6.3 %all-to-all-start.3 = ((bf16[8,2,16384]{2,1,0:T(2,128)(2,1)}), bf16[8,2,16384]{2,1,0:T(2,128)(2,1)S(1)}, u32[]{:S(2)}, u32[]{:S(2)}) async-start(bf16[8,2,16384]{2,1,0:T(2,128)(2,1)} %reshape.190), calls=%async_computation.3 | async-start | bytes 1048576 | tf_op jit(solution)/shard_map/all_to_all | solution.py:112
  17.8 74.8 %all-gather = bf16[32,34,256]{2,1,0:T(8,128)(2,1)S(1)} all-gather(bf16[1,34,256]{2,1,0:T(8,128)(2,1)} %bitcast.83), channel_id=1, replica_groups=mesh['blk'=8,'tenant'=4] {'blk','tenant'}, dimensions={0}, use_global_device_ids=true | all-gather | bytes 574464 | tf_op jit(solution)/shard_map/all_gather | solution.py:51
  93.4 1.3 copy.41
  95.0 3.7 all-to-all-start
  98.8 62.4 %while.12 = (s32[]{:T(128)}, bf16[2176,32]{1,0:T(8,128)(2,1)S(1)}, s32[35,2]{0,1:T(2,128)S(1)}, bf16[35,63,32]{2,1,0:T(8,128)(2,1)}, s32[]{:T(128)}) while((s32[]{:T(128)}, bf16[2176,32]{1,0:T(8,128)(2,1)S(1)}, s32[35,2]{0,1:T(2,128)S(1)}, bf16[35,63,32]{2,1,0:T(8,128)(2,1)}, s32[]{:T(128)}) %tuple.44), condition=%wide.while_cond, body=%wide.while_body.sunk | while | flops 2 | bytes 21529 | solution.py:21
  99.4 1.2 bitcast_dynamic-update-slice_fusion.2
  101.2 1.2 bitcast_dynamic-update-slice_fusion.2
  102.9 1.2 bitcast_dynamic-update-slice_fusion.2
  104.7 1.2 bitcast_dynamic-update-slice_fusion.2
  106.5 1.2 bitcast_dynamic-update-slice_fusion.2
  108.3 1.2 bitcast_dynamic-update-slice_fusion.2
  110.1 1.2 bitcast_dynamic-update-slice_fusion.2
  111.9 1.2 bitcast_dynamic-update-slice_fusion.2
  113.6 1.2 bitcast_dynamic-update-slice_fusion.2
  115.4 1.2 bitcast_dynamic-update-slice_fusion.2
  117.2 1.2 bitcast_dynamic-update-slice_fusion.2
  119.0 1.2 bitcast_dynamic-update-slice_fusion.2
  120.8 1.2 bitcast_dynamic-update-slice_fusion.2
  122.6 1.2 bitcast_dynamic-update-slice_fusion.2
  124.3 1.2 bitcast_dynamic-update-slice_fusion.2
  126.1 1.2 bitcast_dynamic-update-slice_fusion.2
  127.9 1.2 bitcast_dynamic-update-slice_fusion.2
  129.7 1.2 bitcast_dynamic-update-slice_fusion.2
  131.5 1.2 bitcast_dynamic-update-slice_fusion.2
  133.3 1.2 bitcast_dynamic-update-slice_fusion.2
  135.1 1.2 bitcast_dynamic-update-slice_fusion.2
  136.8 1.2 bitcast_dynamic-update-slice_fusion.2
  138.6 1.2 bitcast_dynamic-update-slice_fusion.2
  140.4 1.2 bitcast_dynamic-update-slice_fusion.2
  142.2 1.2 bitcast_dynamic-update-slice_fusion.2
  144.0 1.2 bitcast_dynamic-update-slice_fusion.2
  145.8 1.2 bitcast_dynamic-update-slice_fusion.2
  147.5 1.2 bitcast_dynamic-update-slice_fusion.2
  149.3 1.2 bitcast_dynamic-update-slice_fusion.2
  151.1 1.2 bitcast_dynamic-update-slice_fusion.2
  152.9 1.2 bitcast_dynamic-update-slice_fusion.2
  154.7 1.2 bitcast_dynamic-update-slice_fusion.2
  156.5 1.2 bitcast_dynamic-update-slice_fusion.2
  158.2 1.2 bitcast_dynamic-update-slice_fusion.2
  160.0 1.2 bitcast_dynamic-update-slice_fusion.2
  161.2 2.3 rev.6
  163.8 4.7 %tile.4 = bf16[35,32,32,63]{3,2,1,0:T(8,128)(2,1)} broadcast(bf16[35,32,63]{2,1,0:T(8,128)(2,1)S(1)} %copy.40), dimensions={0,1,3} | broadcast | bytes 4656960 | tf_op jit(solution)/shard_map/vmap()/tile | solution.py:13
  168.6 16.1 %tile.10 = bf16[35,32,2016]{2,1,0:T(8,128)(2,1)} reshape(bf16[35,32,32,63]{3,2,1,0:T(8,128)(2,1)} %tile.4) | data formatting | bytes 9031680 | tf_op jit(solution)/shard_map/vmap()/tile | solution.py:13
  184.7 6.9 %slice.19 = bf16[35,32,1984]{2,1,0:T(8,128)(2,1)} slice(bf16[35,32,2016]{2,1,0:T(8,128)(2,1)} %tile.10), slice={[0:35], [0:32], [31:2015]} | slice | bytes 8888320 | tf_op jit(solution)/shard_map/vmap()/slice | solution.py:14
  191.6 31.4 %reshape.159 = bf16[35,32,32,62]{3,2,1,0:T(8,128)(2,1)} reshape(bf16[35,32,1984]{2,1,0:T(8,128)(2,1)} %slice.19) | data formatting | bytes 8888320 | tf_op jit(solution)/shard_map/vmap()/reshape | solution.py:15
  223.0 14.3 %copy.44 = bf16[35,32,32,32]{0,2,3,1:T(8,128)(2,1)} copy(bf16[35,32,32,32]{3,2,1,0:T(8,128)(2,1)} %bitcast.75) | data formatting | bytes 4587520 | tf_op jit(solution)/shard_map/while | solution.py:35
  237.3 66.1 %all-gather.1 = bf16[32,1,128]{2,1,0:T(2,128)(2,1)S(1)} all-gather(bf16[1,1,128]{2,1,0:T(2,128)(2,1)S(1)} %bitcast.86), channel_id=1, replica_groups=mesh['blk'=8,'tenant'=4] {'blk','tenant'}, dimensions={0}, use_global_device_ids=true | all-gather | bytes 8448 | tf_op jit(solution)/shard_map/all_gather | solution.py:52
  304.3 3.6 all-to-all-start.1
  308.7 4.8 %all-to-all-done.1 = bf16[8,8,512]{2,0,1:T(8,128)(2,1)S(1)} async-done(((bf16[8,8,512]{2,0,1:T(8,128)(2,1)}), bf16[8,8,512]{2,0,1:T(8,128)(2,1)S(1)}, u32[]{:S(2)}, u32[]{:S(2)}) %all-to-all-start.1) | async-done | bytes 65568 | tf_op jit(solution)/shard_map/all_to_all | solution.py:62
  314.6 4.8 %reshape.160 = bf16[34,32,32,16]{1,0,3,2:T(8,128)(2,1)} reshape(bf16[1088,512]{0,1:T(8,128)(2,1)S(1)} %copy.43) | data formatting | bytes 2228224 | tf_op jit(solution)/shard_map/reshape | solution.py:85
  319.4 20.3 %rev.7 = bf16[34,32,32,16]{1,0,3,2:T(8,128)(2,1)} reverse(bf16[34,32,32,16]{1,0,3,2:T(8,128)(2,1)} %reshape.160), dimensions={0} | reverse | bytes 2228224 | tf_op jit(solution)/shard_map/rev | solution.py:85
  339.7 8.7 %copy.45 = bf16[34,32,32,16]{0,3,1,2:T(8,128)(2,1)} copy(bf16[34,32,32,16]{1,0,3,2:T(8,128)(2,1)} %rev.7) | data formatting | bytes 2228224 | tf_op jit(solution)/shard_map/while | solution.py:35
  348.4 29.6 %while.11 = (s32[]{:T(128)}, f32[2,32,32,16]{1,0,3,2:T(2,128)S(1)}, s32[2]{0:T(128)S(1)}, bf16[35,32,32,32]{0,2,3,1:T(8,128)(2,1)}, bf16[34,32,32,16]{0,3,1,2:T(8,128)(2,1)}, /*index=5*/s32[]{:T(128)}, s32[]{:T(128)}, s32[]{:T(128)}) while((s32[]{:T(128)}, f32[2,32,32,16]{1,0,3,2:T(2,128)S(1)}, s32[2]{0:T(128)S(1)}, ...), condition=%wide.region_1.2_spmd, body=%wide.region_0.1_spmd.sunk | while | flops 35651588 | bytes 3604619 | solution.py:35
  350.7 7.0 %fusion.17 = f32[32,32,16,1]{1,2,3,0:T(8,128)S(1)} fusion(bf16[34,32,32,16]{0,3,1,2:T(8,128)(2,1)} %get-tuple-element.175, bf16[35,32,32,32]{0,2,3,1:T(8,128)(2,1)} %get-tuple-element.174, s32[]{:T(128)S(6)} %select_n.48), kind=kOutput, calls=%fused_computation.clone.1 | convolution fusion | flops 35651584 | bytes 3473412 | tf_op jit(solution)/shard_map/while/body/eval_jaxpr/mgab,mbgc->agc/dot_general | solution.py:31
  357.7 5.5 %dynamic_update_slice.9 = f32[2,32,32,16]{1,0,3,2:T(2,128)S(1)} dynamic-update-slice(f32[2,32,32,16]{1,0,3,2:T(2,128)S(1)} %get-tuple-element.164, f32[1,32,32,16]{1,0,3,2:T(1,128)S(1)} %bitcast.76, s32[]{:T(128)} %get-tuple-element.163, s32[]{:T(128)} %constant.20.clone.1..sunk, s32[]{:T(128)} %constant.20.clone.1..sunk, s32[]{:T(128)} %constant.20.clone.1..sunk) | dynamic-update-slice | bytes 131076 | tf_op jit(solution)/shard_map/while/body/jit(dynamic_update_index_in_dim)/dynamic_update_slice | solution.py:35
  365.5 7.0 %fusion.17 = f32[32,32,16,1]{1,2,3,0:T(8,128)S(1)} fusion(bf16[34,32,32,16]{0,3,1,2:T(8,128)(2,1)} %get-tuple-element.175, bf16[35,32,32,32]{0,2,3,1:T(8,128)(2,1)} %get-tuple-element.174, s32[]{:T(128)S(6)} %select_n.48), kind=kOutput, calls=%fused_computation.clone.1 | convolution fusion | flops 35651584 | bytes 3473412 | tf_op jit(solution)/shard_map/while/body/eval_jaxpr/mgab,mbgc->agc/dot_general | solution.py:31
  372.5 5.5 %dynamic_update_slice.9 = f32[2,32,32,16]{1,0,3,2:T(2,128)S(1)} dynamic-update-slice(f32[2,32,32,16]{1,0,3,2:T(2,128)S(1)} %get-tuple-element.164, f32[1,32,32,16]{1,0,3,2:T(1,128)S(1)} %bitcast.76, s32[]{:T(128)} %get-tuple-element.163, s32[]{:T(128)} %constant.20.clone.1..sunk, s32[]{:T(128)} %constant.20.clone.1..sunk, s32[]{:T(128)} %constant.20.clone.1..sunk) | dynamic-update-slice | bytes 131076 | tf_op jit(solution)/shard_map/while/body/jit(dynamic_update_index_in_dim)/dynamic_update_slice | solution.py:35
  378.3 1.2 slice_bitcast_fusion
  386.1 3.4 all-to-all-start.2
  390.9 5.3 %all-to-all-done.2 = f32[8,8,512]{2,1,0:T(8,128)S(1)} async-done(((f32[8,8,512]{2,1,0:T(8,128)}), f32[8,8,512]{2,1,0:T(8,128)S(1)}, u32[]{:S(2)}, u32[]{:S(2)}) %all-to-all-start.2) | async-done | bytes 131104 | tf_op jit(solution)/shard_map/all_to_all | solution.py:90
  396.2 1.5 multiply_convert_fusion
  (129 shorter events, 37.8 us)
Async XLA Ops:
  0.6 92.8 %copy-start = (bf16[1,128,4096]{2,1,0:T(8,128)(2,1)S(1)}, bf16[1,128,4096]{2,1,0:T(8,128)(2,1)}, u32[]{:S(2)}) copy-start(bf16[1,128,4096]{2,1,0:T(8,128)(2,1)} %param.10) | copy-start | bytes 3145732
  11.4 83.6 %all-to-all-start.3 = ((bf16[8,2,16384]{2,1,0:T(2,128)(2,1)}), bf16[8,2,16384]{2,1,0:T(2,128)(2,1)S(1)}, u32[]{:S(2)}, u32[]{:S(2)}) async-start(bf16[8,2,16384]{2,1,0:T(2,128)(2,1)} %reshape.190), calls=%async_computation.3 | async-start | bytes 1048576 | tf_op jit(solution)/shard_map/all_to_all | solution.py:112
  95.0 209.3 %all-to-all-start = ((bf16[128,8,512]{0,2,1:T(8,128)(2,1)}), bf16[128,8,512]{0,2,1:T(8,128)(2,1)S(1)}, u32[]{:S(2)}, u32[]{:S(2)}) async-start(bf16[128,8,512]{0,2,1:T(8,128)(2,1)} %bitcast.8), calls=%async_computation | async-start | bytes 2097152 | tf_op jit(solution)/shard_map/all_to_all | solution.py:61
  223.0 14.3 %copy-start.4 = (bf16[128]{0:T(256)(128)(2,1)S(1)}, bf16[128]{0:T(256)(128)(2,1)}, u32[]{:S(2)}) copy-start(bf16[128]{0:T(256)(128)(2,1)} %param.15) | copy-start | bytes 772
  223.0 80.4 %copy-start.3 = (s32[1,8,1]{1,2,0:T(1,128)S(1)}, s32[1,8,1]{1,2,0:T(1,128)}, u32[]{:S(2)}) copy-start(s32[1,8,1]{1,2,0:T(1,128)} %param.17) | copy-start | bytes 100
  304.3 9.2 %all-to-all-start.1 = ((bf16[8,8,512]{2,0,1:T(8,128)(2,1)}), bf16[8,8,512]{2,0,1:T(8,128)(2,1)S(1)}, u32[]{:S(2)}, u32[]{:S(2)}) async-start(bf16[8,8,512]{2,0,1:T(8,128)(2,1)} %bitcast.11), calls=%async_computation.1 | async-start | bytes 131072 | tf_op jit(solution)/shard_map/all_to_all | solution.py:62
  339.7 8.7 %copy-start.1 = (f32[2,32,32,16]{1,0,3,2:T(2,128)S(1)}, f32[2,32,32,16]{1,0,3,2:T(2,128)}, u32[]{:S(2)}) copy-start(f32[2,32,32,16]{1,0,3,2:T(2,128)} %custom-call.1) | copy-start | bytes 393220
  378.0 18.2 %copy-start.2 = (bf16[1,8,4096]{2,1,0:T(8,128)(2,1)S(1)}, bf16[1,8,4096]{2,1,0:T(8,128)(2,1)}, u32[]{:S(2)}) copy-start(bf16[1,8,4096]{2,1,0:T(8,128)(2,1)} %param.11) | copy-start | bytes 196612
  386.1 10.1 %all-to-all-start.2 = ((f32[8,8,512]{2,1,0:T(8,128)}), f32[8,8,512]{2,1,0:T(8,128)S(1)}, u32[]{:S(2)}, u32[]{:S(2)}) async-start(f32[8,8,512]{2,1,0:T(8,128)} %constant_dynamic-update-slice_fusion), calls=%async_computation.2 | async-start | bytes 262144 | tf_op jit(solution)/shard_map/all_to_all | solution.py:90
